TPU v7x, 32 devices: a whole 2x2x4 slice. The times are simulated.
32 devices in a mesh: ep: 8 (over z, x), tp: 4 (over y, core).
Axes of the slice: x: 2, y: 2, z: 4, core: 2. Of those that a mesh axis runs over, the one named last changes fastest.
Arguments:
- tokens: bfloat16 [2, 1024, 4096], P(None, 'ep', 'tp'), may hold values from -6 to 6
- expert_ids: int32 [2, 1024, 8], P(None, 'ep'), may hold values from 0 to 31, all different within a row; in each aligned block of 128 rows (0 to 127, 128 to 255, ..., all dimensions but the last counted through in order) at most 40 rows name the same one
- route_weight: float32 [2, 1024, 8], P(None, 'ep'), may hold values from 0.1 to 1
- gate_weight: bfloat16 [32, 1536, 4096], P('ep', 'tp'), may hold values from -0.09375 to 0.09375
- up_weight: bfloat16 [32, 1536, 4096], P('ep', 'tp'), may hold values from -0.09375 to 0.09375
- down_weight: bfloat16 [32, 1536, 4096], P('ep', None, 'tp'), may hold values from -0.15625 to 0.15625
- home_slot: int32 [32], replicated, may hold values from 0 to 31, as said below
- spare_expert: int32 [8], replicated, may hold values from 0 to 31, as said below
Outputs:
- mixed: bfloat16 [2, 1024, 4096], P(None, 'ep', 'tp')
- spare_gate: bfloat16 [8, 1536, 4096], P('ep', 'tp')
- spare_up: bfloat16 [8, 1536, 4096], P('ep', 'tp')
- spare_down: bfloat16 [8, 1536, 4096], P('ep', None, 'tp')
Inputs may be any that keep to these rules, and one draw needn't show every extreme that they name: `home_slot`: a permutation; slot s belongs to ep index s // 4. `spare_expert`: names at most 6 distinct experts, whose home slots lie on distinct ep indices; entry d never names an expert whose home slot lies on ep index d. `expert_ids`: each token names 8 distinct experts; in each micro-step the 128 tokens of one ep index name one expert at most 40 times.
All inputs are finite; a program needn't handle non-finite values.
Results may differ from a plain program's by a relative error of at most 0.0058.
Values may be sent and summed in bfloat16 or wider, within the bound.
No kernel may reach another device: no remote copies, remote signals or barrier semaphores. Data moves between devices by JAX's collectives and lax.ppermute only.
A program may use at most 192 MiB of HBM per device.

v0:
```python
import jax
import jax.numpy as jnp
from jax import lax
from jax.sharding import PartitionSpec as P

TOP = 8
STEPS = 2


def slot_targets(expert_pick, home_slot, capacity):
    count_all = home_slot.shape[0]
    expert_iota = lax.iota(jnp.int32, count_all)
    slot_pick = jnp.sum(jnp.where(expert_pick[..., None] == expert_iota, home_slot, 0), axis=-1)
    pair_shape = expert_pick.shape[:-2] + (expert_pick.shape[-2] * expert_pick.shape[-1],)
    pair_slot = slot_pick.reshape(pair_shape)
    one_hot = (pair_slot[..., None] == expert_iota).astype(jnp.int32)
    earlier = jnp.cumsum(one_hot, axis=-2) - one_hot
    position = jnp.sum(earlier * one_hot, axis=-1)
    return (pair_slot * capacity + position).reshape(expert_pick.shape)


def run_steps(tokens, expert_pick, route_weight, gate_weight, up_weight, down_weight, home_slot):
    batches = tokens.shape[0]
    tok_count = tokens.shape[1]
    width_local = tokens.shape[2]
    experts_all = home_slot.shape[0]
    local_count = gate_weight.shape[0]
    owners = experts_all // local_count
    capacity = tok_count * TOP * 5 // (4 * experts_all)
    slot_rows = local_count * capacity
    total_rows = experts_all * capacity
    own_target = slot_targets(expert_pick, home_slot, capacity)
    placing = jnp.any(own_target[..., None] == lax.iota(jnp.int32, total_rows), axis=2).astype(
        jnp.bfloat16
    )
    outgoing = jnp.einsum(
        "btr,btd->brd", placing, tokens, preferred_element_type=jnp.float32
    ).astype(jnp.bfloat16)
    outgoing = outgoing.reshape(batches, owners, slot_rows, width_local)
    arrived = lax.all_to_all(outgoing, "ep", split_axis=1, concat_axis=1, tiled=True)
    piece = lax.all_gather(arrived, "tp", axis=3, tiled=True)
    piece_rows = piece.reshape(batches, owners, local_count, capacity, piece.shape[3])
    gate_add = jnp.einsum(
        "bsecd,efd->bsecf", piece_rows, gate_weight, preferred_element_type=jnp.float32
    )
    up_add = jnp.einsum(
        "bsecd,efd->bsecf", piece_rows, up_weight, preferred_element_type=jnp.float32
    )
    hidden = (jax.nn.silu(gate_add) * up_add).astype(jnp.bfloat16)
    results = jnp.einsum(
        "bsecf,efd->bsecd",
        lax.all_gather(hidden, "tp", axis=4, tiled=True),
        down_weight,
        preferred_element_type=jnp.float32,
    ).astype(jnp.bfloat16)
    results = results.reshape(batches, owners, slot_rows, width_local)
    returned = lax.all_to_all(results, "ep", split_axis=1, concat_axis=1, tiled=True)
    returned = returned.reshape(batches, total_rows, width_local)
    flat_target = own_target.reshape(batches, tok_count * own_target.shape[2])
    picked_rows = jnp.take_along_axis(returned, flat_target[..., None], axis=1)
    picked_rows = picked_rows.reshape(batches, tok_count, own_target.shape[2], width_local).astype(
        jnp.float32
    )
    mixed = jnp.sum(picked_rows * route_weight[..., None], axis=2)
    return mixed.astype(jnp.bfloat16)


def move_spares(gate_weight, up_weight, down_weight, home_slot, spare_expert):
    local_count = gate_weight.shape[0]
    experts_all = home_slot.shape[0]
    owners = spare_expert.shape[0]
    own_index = lax.axis_index("ep")
    expert_iota = lax.iota(jnp.int32, experts_all)
    spare_slot = jnp.sum(jnp.where(spare_expert[:, None] == expert_iota, home_slot, 0), axis=1)
    spare_home = spare_slot // local_count
    own_slot = jnp.max(jnp.where(spare_home == own_index, spare_slot % local_count, 0))
    gate_part = lax.dynamic_index_in_dim(gate_weight, own_slot, 0, keepdims=False)
    up_part = lax.dynamic_index_in_dim(up_weight, own_slot, 0, keepdims=False)
    down_part = lax.dynamic_index_in_dim(down_weight, own_slot, 0, keepdims=False)
    gate_pieces = gate_part.reshape(gate_part.shape[0], owners, gate_part.shape[1] // owners)
    up_pieces = up_part.reshape(up_part.shape[0], owners, up_part.shape[1] // owners)
    down_pieces = down_part.reshape(down_part.shape[0], owners, down_part.shape[1] // owners)
    spread_gate, spread_up, spread_down = (
        lax.all_to_all(gate_pieces, "ep", split_axis=1, concat_axis=1, tiled=True),
        lax.all_to_all(up_pieces, "ep", split_axis=1, concat_axis=1, tiled=True),
        lax.all_to_all(down_pieces, "ep", split_axis=1, concat_axis=1, tiled=True),
    )
    chosen_gate = jnp.take(spread_gate, spare_home, axis=1)
    chosen_up = jnp.take(spread_up, spare_home, axis=1)
    chosen_down = jnp.take(spread_down, spare_home, axis=1)
    landed_gate, landed_up, landed_down = (
        lax.all_to_all(chosen_gate, "ep", split_axis=1, concat_axis=1, tiled=True),
        lax.all_to_all(chosen_up, "ep", split_axis=1, concat_axis=1, tiled=True),
        lax.all_to_all(chosen_down, "ep", split_axis=1, concat_axis=1, tiled=True),
    )
    spare_gate = landed_gate.reshape(1, gate_part.shape[0], gate_part.shape[1])
    spare_up = landed_up.reshape(1, up_part.shape[0], up_part.shape[1])
    spare_down = landed_down.reshape(1, down_part.shape[0], down_part.shape[1])
    return (spare_gate, spare_up, spare_down)


def shards(
    tokens, expert_ids, route_weight, gate_weight, up_weight, down_weight, home_slot, spare_expert
):
    spare_gate, spare_up, spare_down = move_spares(
        gate_weight, up_weight, down_weight, home_slot, spare_expert
    )
    outputs = [
        run_steps(
            tokens[step_index : step_index + 1],
            expert_ids[step_index : step_index + 1],
            route_weight[step_index : step_index + 1],
            gate_weight,
            up_weight,
            down_weight,
            home_slot,
        )
        for step_index in range(STEPS)
    ]
    mixed = jnp.concatenate(outputs, axis=0)
    return (mixed, spare_gate, spare_up, spare_down)


def solution(mesh):
    placed = (
        P(None, "ep", "tp"),
        P(None, "ep", None),
        P(None, "ep", None),
        P("ep", "tp", None),
        P("ep", "tp", None),
        P("ep", None, "tp"),
        P(),
        P(),
    )
    return jax.shard_map(
        shards,
        mesh=mesh,
        in_specs=placed,
        out_specs=(
            P(None, "ep", "tp"),
            P("ep", "tp", None),
            P("ep", "tp", None),
            P("ep", None, "tp"),
        ),
        check_vma=False,
    )
```

profile of v0, /device:TPU:0, one launch (start us, length us, event | category | flops | bytes accessed | tf_op | source)
XLA Modules:
  0.0 761.7 jit_solution(297695629966626307)
XLA Ops:
  9.0 9.0 %reduce-window.14 = s32[1,32,8,128]{3,2,1,0:T(8,128)S(1)} reduce-window(s32[1,32,8,128]{3,2,1,0:T(8,128)S(1)} %bitcast.226, s32[]{:T(128)} %constant.82.clone.1), window={size=1x1x1x128 pad=0_0x0_0x0_0x127_0}, to_apply=%region_1.2 | reduce-window | flops 4161536 | bytes 262148 | tf_op jit(solution)/shard_map/reduce-window
  18.4 9.0 %reduce-window.16 = s32[1,32,8,128]{3,2,1,0:T(8,128)S(1)} reduce-window(s32[1,32,8,128]{3,2,1,0:T(8,128)S(1)} %bitcast.227, s32[]{:T(128)} %constant.82.clone.1), window={size=1x1x1x128 pad=0_0x0_0x0_0x127_0}, to_apply=%region_7.9 | reduce-window | flops 4161536 | bytes 262148 | tf_op jit(solution)/shard_map/reduce-window.2
  31.4 66.7 %all_to_all.50 = bf16[1,8,160,1024]{3,2,0,1:T(8,128)(2,1)} all-to-all(bf16[1,8,160,1024]{3,2,0,1:T(8,128)(2,1)S(1)} %bitcast.223), channel_id=1, replica_groups=mesh['ep'=8,'tp'=4] {'ep'}, dimensions={1} | all-to-all | bytes 5242880 | tf_op jit(solution)/shard_map/all_to_all | solution.py:40
  102.2 4.6 all-to-all-start.2
  109.7 6.8 constant_dynamic-slice_fusion.1
  122.7 42.7 %all-to-all-done.2 = bf16[1,8,160,1024]{3,2,0,1:T(8,128)(2,1)} async-done(((bf16[1,8,160,1024]{3,2,0,1:T(8,128)(2,1)}), bf16[1,8,160,1024]{3,2,0,1:T(8,128)(2,1)}, u32[]{:S(2)}, u32[]{:S(2)}) %all-to-all-start.2) | async-done | bytes 2621472 | tf_op jit(solution)/shard_map/all_to_all | solution.py:40
  169.1 4.6 copy.130
  173.7 4.6 copy.118
  178.3 61.6 %all-to-all-done.4 = bf16[384,8,512]{2,0,1:T(8,128)(2,1)S(1)} async-done(((bf16[384,8,512]{2,0,1:T(8,128)(2,1)}), bf16[384,8,512]{2,0,1:T(8,128)(2,1)S(1)}, u32[]{:S(2)}, u32[]{:S(2)}) %all-to-all-start.4) | async-done | bytes 3145760 | tf_op jit(solution)/shard_map/all_to_all | solution.py:84
  251.9 4.6 copy.121
  256.5 59.7 %all-to-all-done.6 = bf16[384,8,512]{2,0,1:T(8,128)(2,1)} async-done(((bf16[384,8,512]{2,0,1:T(8,128)(2,1)}), bf16[384,8,512]{2,0,1:T(8,128)(2,1)}, u32[]{:S(2)}, u32[]{:S(2)}) %all-to-all-start.6) | async-done | bytes 3145760 | tf_op jit(solution)/shard_map/all_to_all | solution.py:85
  328.5 6.2 select_bitcast_fusion
  334.7 56.1 %all-to-all-done.8 = bf16[1536,8,128]{2,0,1:T(8,128)(2,1)S(1)} async-done(((bf16[1536,8,128]{2,0,1:T(8,128)(2,1)}), bf16[1536,8,128]{2,0,1:T(8,128)(2,1)S(1)}, u32[]{:S(2)}, u32[]{:S(2)}) %all-to-all-start.8) | async-done | bytes 3145760 | tf_op jit(solution)/shard_map/all_to_all | solution.py:86
  390.7 74.8 %all_to_all.51 = bf16[384,8,512]{2,0,1:T(8,128)(2,1)} all-to-all(bf16[384,8,512]{2,0,1:T(8,128)(2,1)} %get-tuple-element.35), channel_id=1, replica_groups=mesh['ep'=8,'tp'=4] {'ep'}, dimensions={1} | all-to-all | bytes 6291456 | tf_op jit(solution)/shard_map/all_to_all | solution.py:92
  469.4 15.1 %fusion.10 = f32[4,8,40,384]{3,2,1,0:T(8,128)} fusion(bf16[4,384,4096]{2,1,0:T(8,128)(2,1)} %param.15, bf16[8,4,40,4096]{3,2,1,0:T(8,128)(2,1)} %bitcast.234), kind=kOutput, calls=%fused_computation.15 | convolution fusion | flops 4026531840 | bytes 25034752 | tf_op jit(solution)/shard_map/bsecd,efd->bsecf/dot_general | solution.py:43
  484.5 15.3 %fusion.31 = bf16[1,8,4,40,384]{4,3,1,2,0:T(8,128)(2,1)} fusion(f32[4,8,40,384]{3,2,1,0:T(8,128)} %fusion.10, bf16[4,384,4096]{2,1,0:T(8,128)(2,1)} %param.16, bf16[8,4,40,4096]{3,2,1,0:T(8,128)(2,1)} %bitcast.235), kind=kOutput, calls=%fused_computation.43 | convolution fusion | flops 4029480960 | bytes 26017792 | tf_op jit(solution)/shard_map/bsecd,efd->bsecf/dot_general | solution.py:46
  508.3 31.0 %all-to-all-done.7 = bf16[384,8,512]{2,0,1:T(8,128)(2,1)S(1)} async-done(((bf16[384,8,512]{2,0,1:T(8,128)(2,1)}), bf16[384,8,512]{2,0,1:T(8,128)(2,1)S(1)}, u32[]{:S(2)}, u32[]{:S(2)}) %all-to-all-start.7) | async-done | bytes 3145760 | tf_op jit(solution)/shard_map/all_to_all | solution.py:93
  545.7 14.2 %fusion.8 = f32[4,8,40,384]{3,2,1,0:T(8,128)S(1)} fusion(bf16[4,384,4096]{2,1,0:T(8,128)(2,1)} %param.15, bf16[8,4,40,4096]{3,2,1,0:T(8,128)(2,1)} %bitcast.236), kind=kOutput, calls=%fused_computation.13 | convolution fusion | flops 4026531840 | bytes 25034752 | tf_op jit(solution)/shard_map/bsecd,efd->bsecf/dot_general | solution.py:43
  559.8 15.0 %fusion.30 = bf16[1,8,4,40,384]{4,3,1,2,0:T(8,128)(2,1)} fusion(f32[4,8,40,384]{3,2,1,0:T(8,128)S(1)} %fusion.8, bf16[4,384,4096]{2,1,0:T(8,128)(2,1)} %param.16, bf16[8,4,40,4096]{3,2,1,0:T(8,128)(2,1)} %bitcast.237), kind=kOutput, calls=%fused_computation.41 | convolution fusion | flops 4029480960 | bytes 26017792 | tf_op jit(solution)/shard_map/bsecd,efd->bsecf/dot_general | solution.py:46
  574.9 10.0 %convert_bitcast_fusion.1 = bf16[1,8,4,40,1024]{4,3,1,2,0:T(8,128)(2,1)S(1)} fusion(bf16[4,1536,1024]{2,1,0:T(8,128)(2,1)} %param.17, bf16[1,8,4,40,1536]{4,3,1,2,0:T(8,128)(2,1)} %all-gather.7.cloned.1.call-done), kind=kOutput, calls=%fused_computation.37 | convolution fusion | flops 4027842560 | bytes 19136512 | tf_op jit(solution)/shard_map/bsecf,efd->bsecd/dot_general | solution.py:50
  586.7 28.8 %all-to-all-done.9 = bf16[1536,8,128]{2,0,1:T(8,128)(2,1)} async-done(((bf16[1536,8,128]{2,0,1:T(8,128)(2,1)}), bf16[1536,8,128]{2,0,1:T(8,128)(2,1)}, u32[]{:S(2)}, u32[]{:S(2)}) %all-to-all-start.9) | async-done | bytes 3145760 | tf_op jit(solution)/shard_map/all_to_all | solution.py:94
  619.5 10.0 %convert_bitcast_fusion = bf16[1,8,4,40,1024]{4,3,1,2,0:T(8,128)(2,1)S(1)} fusion(bf16[4,1536,1024]{2,1,0:T(8,128)(2,1)} %param.17, bf16[1,8,4,40,1536]{4,3,1,2,0:T(8,128)(2,1)} %all-gather.11.cloned.1.call-done), kind=kOutput, calls=%fused_computation.36 | convolution fusion | flops 4027842560 | bytes 19136512 | tf_op jit(solution)/shard_map/bsecf,efd->bsecd/dot_general | solution.py:50
  631.3 47.8 %all-to-all-done.1 = bf16[1,8,160,1024]{3,2,0,1:T(8,128)(2,1)S(1)} async-done(((bf16[1,8,160,1024]{3,2,0,1:T(8,128)(2,1)}), bf16[1,8,160,1024]{3,2,0,1:T(8,128)(2,1)S(1)}, u32[]{:S(2)}, u32[]{:S(2)}) %all-to-all-start.1) | async-done | bytes 2621472 | tf_op jit(solution)/shard_map/all_to_all | solution.py:57
  684.2 4.6 copy.116
  688.8 4.6 copy.123
  693.4 4.6 copy.119
  698.1 4.6 copy.124
  702.7 4.6 copy.122
  707.4 4.6 copy.125
  712.0 5.4 gather_fusion.1
  717.3 25.1 %all-to-all-done.3 = bf16[1,8,160,1024]{3,2,0,1:T(8,128)(2,1)} async-done(((bf16[1,8,160,1024]{3,2,0,1:T(8,128)(2,1)}), bf16[1,8,160,1024]{3,2,0,1:T(8,128)(2,1)}, u32[]{:S(2)}, u32[]{:S(2)}) %all-to-all-start.3) | async-done | bytes 2621472 | tf_op jit(solution)/shard_map/all_to_all | solution.py:57
  742.5 8.2 %gather_fusion.2 = bf16[1024,1024]{1,0:T(8,128)(2,1)} fusion(bf16[1280,1024]{1,0:T(8,128)(2,1)} %bitcast.67, s32[1024]{0:T(1024)S(1)} %broadcast_clamp_fusion), kind=kCustom, calls=%fused_computation.2.clone | custom fusion | bytes 4198400 | tf_op jit(solution)/shard_map/jit(take_along_axis)/gather | solution.py:60
  (106 shorter events, 80.4 us)
Async XLA Ops:
  7.2 23.3 %copy-start.5 = (bf16[2,128,1024]{2,1,0:T(8,128)(2,1)S(1)}, bf16[2,128,1024]{2,1,0:T(8,128)(2,1)}, u32[]{:S(2)}) copy-start(bf16[2,128,1024]{2,1,0:T(8,128)(2,1)} %param.12) | copy-start | bytes 1572868
  7.2 462.2 %all-gather.5.cloned.1.call-start = ((), (), s32[]{:S(2)}) async-start(), calls=%async_computation.10 | async-start | bytes 13107200 | tf_op jit(solution)/shard_map/all_gather | solution.py:41
  102.2 4.6 copy-start.7
  102.2 4.6 copy-start.8
  102.2 63.2 %all-to-all-start.2 = ((bf16[1,8,160,1024]{3,2,0,1:T(8,128)(2,1)}), bf16[1,8,160,1024]{3,2,0,1:T(8,128)(2,1)}, u32[]{:S(2)}, u32[]{:S(2)}) async-start(bf16[1,8,160,1024]{3,2,0,1:T(8,128)(2,1)} %bitcast.46), calls=%async_computation.2 | async-start | bytes 5242880 | tf_op jit(solution)/shard_map/all_to_all | solution.py:40
  165.4 74.5 %all-to-all-start.4 = ((bf16[384,8,512]{2,0,1:T(8,128)(2,1)}), bf16[384,8,512]{2,0,1:T(8,128)(2,1)S(1)}, u32[]{:S(2)}, u32[]{:S(2)}) async-start(bf16[384,8,512]{2,0,1:T(8,128)(2,1)} %copy.115), calls=%async_computation.4 | async-start | bytes 6291456 | tf_op jit(solution)/shard_map/all_to_all | solution.py:84
  239.9 1.7 copy-start.2
  241.6 74.6 %all-to-all-start.6 = ((bf16[384,8,512]{2,0,1:T(8,128)(2,1)}), bf16[384,8,512]{2,0,1:T(8,128)(2,1)}, u32[]{:S(2)}, u32[]{:S(2)}) async-start(bf16[384,8,512]{2,0,1:T(8,128)(2,1)} %copy.118), calls=%async_computation.6 | async-start | bytes 6291456 | tf_op jit(solution)/shard_map/all_to_all | solution.py:85
  246.0 299.6 %all-gather.9.cloned.1.call-start = ((), (), s32[]{:S(2)}) async-start(), calls=%async_computation.12 | async-start | bytes 13107200 | tf_op jit(solution)/shard_map/all_gather | solution.py:41
  316.2 74.5 %all-to-all-start.8 = ((bf16[1536,8,128]{2,0,1:T(8,128)(2,1)}), bf16[1536,8,128]{2,0,1:T(8,128)(2,1)S(1)}, u32[]{:S(2)}, u32[]{:S(2)}) async-start(bf16[1536,8,128]{2,0,1:T(8,128)(2,1)} %copy.121), calls=%async_computation.8 | async-start | bytes 6291456 | tf_op jit(solution)/shard_map/all_to_all | solution.py:86
  390.7 74.8 %copy-start.1 = (bf16[1536,8,128]{2,0,1:T(8,128)(2,1)}, bf16[1536,8,128]{2,0,1:T(8,128)(2,1)S(1)}, u32[]{:S(2)}) copy-start(bf16[1536,8,128]{2,0,1:T(8,128)(2,1)S(1)} %all-to-all-done.8) | copy-start | bytes 9437188
  465.5 73.8 %all-to-all-start.7 = ((bf16[384,8,512]{2,0,1:T(8,128)(2,1)}), bf16[384,8,512]{2,0,1:T(8,128)(2,1)S(1)}, u32[]{:S(2)}, u32[]{:S(2)}) async-start(bf16[384,8,512]{2,0,1:T(8,128)(2,1)} %get-tuple-element.34), calls=%async_computation.7 | async-start | bytes 6291456 | tf_op jit(solution)/shard_map/all_to_all | solution.py:93
  469.2 105.8 %all-gather.7.cloned.1.call-start = ((), (), s32[]{:S(2)}) async-start(), calls=%async_computation.11 | async-start | bytes 4915200 | tf_op jit(solution)/shard_map/all_gather | solution.py:52
  539.3 1.7 copy-start
  540.9 74.6 %all-to-all-start.9 = ((bf16[1536,8,128]{2,0,1:T(8,128)(2,1)}), bf16[1536,8,128]{2,0,1:T(8,128)(2,1)}, u32[]{:S(2)}, u32[]{:S(2)}) async-start(bf16[1536,8,128]{2,0,1:T(8,128)(2,1)} %select_bitcast_fusion.2), calls=%async_computation.9 | async-start | bytes 6291456 | tf_op jit(solution)/shard_map/all_to_all | solution.py:94
  545.4 74.1 %all-gather.11.cloned.1.call-start = ((), (), s32[]{:S(2)}) async-start(), calls=%async_computation.13 | async-start | bytes 4915200 | tf_op jit(solution)/shard_map/all_gather | solution.py:52
  615.6 63.5 %all-to-all-start.1 = ((bf16[1,8,160,1024]{3,2,0,1:T(8,128)(2,1)}), bf16[1,8,160,1024]{3,2,0,1:T(8,128)(2,1)S(1)}, u32[]{:S(2)}, u32[]{:S(2)}) async-start(bf16[1,8,160,1024]{3,2,0,1:T(8,128)(2,1)} %bitcast.222), calls=%async_computation.1 | async-start | bytes 5242880 | tf_op jit(solution)/shard_map/all_to_all | solution.py:57
  631.3 52.4 %copy-start.6 = (f32[2,128,8]{1,2,0:T(8,128)S(1)}, f32[2,128,8]{1,2,0:T(8,128)}, u32[]{:S(2)}) copy-start(f32[2,128,8]{1,2,0:T(8,128)} %param.14) | copy-start | bytes 24580
  679.1 63.4 %all-to-all-start.3 = ((bf16[1,8,160,1024]{3,2,0,1:T(8,128)(2,1)}), bf16[1,8,160,1024]{3,2,0,1:T(8,128)(2,1)}, u32[]{:S(2)}, u32[]{:S(2)}) async-start(bf16[1,8,160,1024]{3,2,0,1:T(8,128)(2,1)} %bitcast.221), calls=%async_computation.3 | async-start | bytes 5242880 | tf_op jit(solution)/shard_map/all_to_all | solution.py:57
  742.5 8.2 %copy-start.3 = (bf16[1024,1024]{1,0:T(8,128)(2,1)S(1)}, bf16[1024,1024]{1,0:T(8,128)(2,1)}, u32[]{:S(2)}) copy-start(bf16[1024,1024]{1,0:T(8,128)(2,1)} %gather_fusion.1) | copy-start | bytes 6291460
  750.7 1.6 copy-start.4
Sparse Core Ops, SparseCore 0:
  98.2 69.2 all-gather.4
  248.4 71.4 all-gather.8
  500.0 34.2 all-gather.6
  575.0 34.2 all-gather.10
where the time goes:
time: 772 us; the launch traced here: 762 us
  waiting for transfers between devices  354 us (46%)
  blocking collectives  141 us (18%)
  local copies, waits for them, and re-layouts  96.8 us (13%)
  matrix products  82.9 us (11%)
  other arithmetic  37.1 us (5%)
  starting transfers between devices  33.3 us (4%)
  between operations  16.6 us (2%)
    all_to_all x1, blocking collectives, move_spares(): lax.all_to_all(chosen_gate, 'ep', split_axis=1, concat_axis=1, tiled=True)  74.8 us
    all_to_all x2, waiting for transfers between devices, run_steps(): lax.all_to_all(results, 'ep', split_axis=1, concat_axis=1, tiled=True)  72.9 us
    all_to_all x1, blocking collectives, run_steps(): lax.all_to_all(outgoing, 'ep', split_axis=1, concat_axis=1, tiled=True)  66.7 us
    all_to_all x1, waiting for transfers between devices, move_spares(): lax.all_to_all(gate_pieces, 'ep', split_axis=1, concat_axis=1, tiled=True)  61.6 us
    all_to_all x1, waiting for transfers between devices, move_spares(): lax.all_to_all(up_pieces, 'ep', split_axis=1, concat_axis=1, tiled=True)  59.7 us
    all_to_all x1, waiting for transfers between devices, move_spares(): lax.all_to_all(down_pieces, 'ep', split_axis=1, concat_axis=1, tiled=True)  56.1 us
    all_to_all x1, waiting for transfers between devices, run_steps(): lax.all_to_all(outgoing, 'ep', split_axis=1, concat_axis=1, tiled=True)  42.7 us
    all_to_all x1, waiting for transfers between devices, move_spares(): lax.all_to_all(chosen_up, 'ep', split_axis=1, concat_axis=1, tiled=True)  31 us
  transfers between devices with their start and end apart: 12, of which 8 were waited for; matrix products, arithmetic and copies ran while one was open for 23% of the time, Pallas kernels for 0%

commit v1 on v0

v1 whole, which is shorter than its diff:
```python
import functools
import math

import jax
import jax.numpy as jnp
from jax import lax
from jax.experimental import pallas as pl
from jax.experimental.pallas import tpu as pltpu
from jax.sharding import PartitionSpec as P

TOP = 8
PACK = 16


def hidden_kernel(tp, group, cap, pos_ref, x_ref, gate_ref, up_ref, out_ref, rows_ref):
    local = rows_ref.shape[0]
    width = x_ref.shape[3]
    block = group * cap
    tall = group * x_ref.shape[2]

    @pl.when(pl.program_id(0) == 0)
    def _():
        def gather(p, carry):
            rows = lax.broadcasted_iota(jnp.int32, (block, tall), 0)
            picks = jnp.concatenate(
                [
                    jnp.where(rows == pos_ref[0, p, e : e + 1, :], 1.0, 0.0).astype(jnp.bfloat16)
                    for e in range(local)
                ],
                axis=0,
            )
            start = pl.multiple_of(p * block, PACK)
            for t in range(tp):
                part = jnp.concatenate(
                    [x_ref[(p * group + j) * tp + t, 0] for j in range(group)], axis=0
                )
                got = jnp.dot(picks, part, preferred_element_type=jnp.float32).astype(jnp.bfloat16)
                for e in range(local):
                    rows_ref[e, pl.ds(start, block), t * width : (t + 1) * width] = got[
                        e * block : (e + 1) * block
                    ]
            return carry

        lax.fori_loop(0, pos_ref.shape[1], gather, 0)

    rows = rows_ref[pl.program_id(0)]
    dims = (((1,), (1,)), ((), ()))
    gate = lax.dot_general(rows, gate_ref[0], dims, preferred_element_type=jnp.float32)
    up = lax.dot_general(rows, up_ref[0], dims, preferred_element_type=jnp.float32)
    out_ref[0] = (gate / (1.0 + jnp.exp(-gate)) * up).astype(out_ref.dtype)


def hidden_units(step, pos, x, gate_weight, up_weight, tp, group, cap):
    local, units, width = gate_weight.shape
    parts, tall = pos.shape[1], pos.shape[3]
    rows = parts * group * cap
    return pl.pallas_call(
        functools.partial(hidden_kernel, tp, group, cap),
        grid=(local,),
        in_specs=[
            pl.BlockSpec((1, parts, local, tall), lambda e: (step, 0, 0, 0)),
            pl.BlockSpec(
                (x.shape[0], 1) + x.shape[2:],
                lambda e: (0, step, 0, 0),
                pipeline_mode=pl.Buffered(1),
            ),
            pl.BlockSpec((1, units, width), lambda e: (e, 0, 0)),
            pl.BlockSpec((1, units, width), lambda e: (e, 0, 0)),
        ],
        out_specs=pl.BlockSpec((1, rows, units), lambda e: (e, 0, 0)),
        out_shape=jax.ShapeDtypeStruct((local, rows, units), jnp.bfloat16),
        scratch_shapes=[pltpu.VMEM((local, rows, width), jnp.bfloat16)],
        compiler_params=pltpu.CompilerParams(vmem_limit_bytes=56 << 20),
        cost_estimate=pl.CostEstimate(
            flops=4 * local * rows * units * width,
            bytes_accessed=4 * local * units * width + 2 * x.size // x.shape[1],
            transcendentals=local * rows * units,
        ),
        name="hidden_units",
    )(pos, x, gate_weight, up_weight)


def combine_kernel(tp, group, cap, has_base, pos_ref, weight_ref, h_ref, down_ref, *refs):
    out_ref, total_ref = refs[1:] if has_base else refs
    expert = pl.program_id(0)
    block = group * cap
    parts, tall, local = pos_ref.shape[1:]
    tokens = tall // group
    h = jnp.concatenate([h_ref[t, 0] for t in range(tp)], axis=1)
    res = jnp.dot(h, down_ref[0], preferred_element_type=jnp.float32).astype(jnp.bfloat16)
    own = lax.broadcasted_iota(jnp.int32, (tall, local), 1) == expert
    for p in range(parts):
        place = jnp.sum(jnp.where(own, pos_ref[0, p], 0), axis=1, keepdims=True)
        weight = jnp.sum(jnp.where(own, weight_ref[0, p], 0.0), axis=1, keepdims=True)
        lanes = lax.broadcasted_iota(jnp.int32, (tall, block), 1)
        picks = jnp.where(lanes == place, 1.0, 0.0).astype(jnp.bfloat16)
        got = weight * jnp.dot(
            picks, res[p * block : (p + 1) * block], preferred_element_type=jnp.float32
        )

        @pl.when(expert == 0)
        def _():
            total_ref[p] = got

        @pl.when(expert > 0)
        def _():
            total_ref[p] += got

    @pl.when(expert == local - 1)
    def _():
        for p in range(parts):
            for j in range(group):
                out_ref[p * group + j, 0] = total_ref[p, j * tokens : (j + 1) * tokens].astype(
                    out_ref.dtype
                )


def combine(step, steps, pos, weight, h, down_weight, group, cap, base):
    tp, local, rows, units = h.shape
    parts, tall = pos.shape[1], pos.shape[2]
    width = down_weight.shape[2]
    tokens = tall // group
    out_block = (parts * group, 1, tokens, width)
    operands = [pos, weight, h, down_weight]
    in_specs = [
        pl.BlockSpec((1, parts, tall, local), lambda e: (step, 0, 0, 0)),
        pl.BlockSpec((1, parts, tall, local), lambda e: (step, 0, 0, 0)),
        pl.BlockSpec((tp, 1, rows, units), lambda e: (0, e, 0, 0)),
        pl.BlockSpec((1, tp * units, width), lambda e: (e, 0, 0)),
    ]
    if base is not None:
        operands.append(base)
        in_specs.append(pl.BlockSpec(memory_space=pl.ANY))
    return pl.pallas_call(
        functools.partial(combine_kernel, tp, group, cap, base is not None),
        grid=(local,),
        in_specs=in_specs,
        out_specs=pl.BlockSpec(out_block, lambda e: (0, step, 0, 0)),
        out_shape=jax.ShapeDtypeStruct((parts * group, steps, tokens, width), jnp.bfloat16),
        scratch_shapes=[pltpu.VMEM((parts, tall, width), jnp.float32)],
        input_output_aliases={} if base is None else {4: 0},
        compiler_params=pltpu.CompilerParams(vmem_limit_bytes=56 << 20),
        cost_estimate=pl.CostEstimate(
            flops=2 * local * rows * tp * units * width,
            bytes_accessed=2 * local * tp * units * width + 2 * h.size,
            transcendentals=0,
        ),
        name="combine",
    )(*operands)


def placing(expert_ids, route_weight, home_slot, local, cap, group):
    experts_all = home_slot.shape[0]
    packed = jnp.concatenate([expert_ids.astype(jnp.float32), route_weight], axis=-1)
    packed = lax.all_gather(packed, "ep")
    ids = packed[..., : expert_ids.shape[-1]].astype(jnp.int32)
    weights = packed[..., expert_ids.shape[-1] :]
    slots = lax.axis_index("ep") * local + lax.iota(jnp.int32, local)
    named = jnp.sum(
        jnp.where(home_slot[None, :] == slots[:, None], lax.iota(jnp.int32, experts_all), 0), axis=1
    )
    match = ids[..., None] == named
    member = jnp.any(match, axis=3)
    weight = jnp.sum(jnp.where(match, weights[..., None], 0.0), axis=3)
    tokens = ids.shape[2]
    earlier = (lax.iota(jnp.int32, tokens)[None, :] < lax.iota(jnp.int32, tokens)[:, None]).astype(
        jnp.bfloat16
    )
    position = jnp.einsum(
        "ut,sbte->sbue", earlier, member.astype(jnp.bfloat16), preferred_element_type=jnp.float32
    ).astype(jnp.int32)
    offset = (lax.iota(jnp.int32, ids.shape[0]) % group * cap)[:, None, None, None]
    position = jnp.where(member, position + offset, -1)
    sources, steps = ids.shape[:2]

    def arrange(v):
        v = v.reshape(sources // group, group, steps, tokens, local)
        return v.transpose(2, 0, 1, 3, 4).reshape(steps, sources // group, group * tokens, local)

    position = arrange(position)
    return position, position.transpose(0, 1, 3, 2), arrange(weight)


def run_steps(tokens, expert_ids, route_weight, gate_weight, up_weight, down_weight, home_slot, tp):
    steps, tok_count = tokens.shape[:2]
    local = gate_weight.shape[0]
    experts_all = home_slot.shape[0]
    cap = tok_count * TOP * 5 // (4 * experts_all)
    group = PACK // math.gcd(PACK, cap)
    x = lax.all_gather(tokens, ("ep", "tp"))
    columns, rows, weight = placing(expert_ids, route_weight, home_slot, local, cap, group)
    out = None
    for step in range(steps):
        h = hidden_units(step, rows, x, gate_weight, up_weight, tp, group, cap)
        h = lax.all_gather(h, "tp")
        out = combine(step, steps, columns, weight, h, down_weight, group, cap, out)
    mixed = lax.psum_scatter(out, "ep", scatter_dimension=0, tiled=True)
    return mixed.reshape(tokens.shape)


def move_spares(gate_weight, up_weight, down_weight, home_slot, spare_expert):
    local_count = gate_weight.shape[0]
    experts_all = home_slot.shape[0]
    owners = spare_expert.shape[0]
    own_index = lax.axis_index("ep")
    expert_iota = lax.iota(jnp.int32, experts_all)
    spare_slot = jnp.sum(jnp.where(spare_expert[:, None] == expert_iota, home_slot, 0), axis=1)
    spare_home = spare_slot // local_count
    own_slot = jnp.max(jnp.where(spare_home == own_index, spare_slot % local_count, 0))
    gate_part = lax.dynamic_index_in_dim(gate_weight, own_slot, 0, keepdims=False)
    up_part = lax.dynamic_index_in_dim(up_weight, own_slot, 0, keepdims=False)
    down_part = lax.dynamic_index_in_dim(down_weight, own_slot, 0, keepdims=False)
    gate_pieces = gate_part.reshape(gate_part.shape[0], owners, gate_part.shape[1] // owners)
    up_pieces = up_part.reshape(up_part.shape[0], owners, up_part.shape[1] // owners)
    down_pieces = down_part.reshape(down_part.shape[0], owners, down_part.shape[1] // owners)
    spread_gate, spread_up, spread_down = (
        lax.all_to_all(gate_pieces, "ep", split_axis=1, concat_axis=1, tiled=True),
        lax.all_to_all(up_pieces, "ep", split_axis=1, concat_axis=1, tiled=True),
        lax.all_to_all(down_pieces, "ep", split_axis=1, concat_axis=1, tiled=True),
    )
    chosen_gate = jnp.take(spread_gate, spare_home, axis=1)
    chosen_up = jnp.take(spread_up, spare_home, axis=1)
    chosen_down = jnp.take(spread_down, spare_home, axis=1)
    landed_gate, landed_up, landed_down = (
        lax.all_to_all(chosen_gate, "ep", split_axis=1, concat_axis=1, tiled=True),
        lax.all_to_all(chosen_up, "ep", split_axis=1, concat_axis=1, tiled=True),
        lax.all_to_all(chosen_down, "ep", split_axis=1, concat_axis=1, tiled=True),
    )
    spare_gate = landed_gate.reshape(1, gate_part.shape[0], gate_part.shape[1])
    spare_up = landed_up.reshape(1, up_part.shape[0], up_part.shape[1])
    spare_down = landed_down.reshape(1, down_part.shape[0], down_part.shape[1])
    return (spare_gate, spare_up, spare_down)


def shards(
    tp, tokens, expert_ids, route_weight, gate_weight, up_weight, down_weight, home_slot, spare_expert
):
    spare_gate, spare_up, spare_down = move_spares(
        gate_weight, up_weight, down_weight, home_slot, spare_expert
    )
    mixed = run_steps(
        tokens, expert_ids, route_weight, gate_weight, up_weight, down_weight, home_slot, tp
    )
    return (mixed, spare_gate, spare_up, spare_down)


def solution(mesh):
    placed = (
        P(None, "ep", "tp"),
        P(None, "ep", None),
        P(None, "ep", None),
        P("ep", "tp", None),
        P("ep", "tp", None),
        P("ep", None, "tp"),
        P(),
        P(),
    )
    return jax.shard_map(
        functools.partial(shards, mesh.shape["tp"]),
        mesh=mesh,
        in_specs=placed,
        out_specs=(
            P(None, "ep", "tp"),
            P("ep", "tp", None),
            P("ep", "tp", None),
            P("ep", None, "tp"),
        ),
        check_vma=False,
    )
```

time: 772 us -> 651 us (0.84); the launches traced: 762 us -> 649 us
  matrix products: 82.9 us -> 0.12 us
  Pallas kernels: 0 us -> 72.4 us
  blocking collectives: 141 us -> 91 us
  other arithmetic: 37.1 us -> 9.74 us
  local copies, waits for them, and re-layouts: 96.8 us -> 75.3 us
    all_to_all x2 -> x0, blocking collectives: 141 us -> none  [the longest x1 74.8 us: move_spares(): lax.all_to_all(chosen_gate, 'ep', split_axis=1, concat_axis=1, tiled=True)]
    all_gather x0 -> x1, blocking collectives: none -> 91 us  [placing(): packed = lax.all_gather(packed, 'ep')]
    dot_general x8 -> x1, matrix products: 82.9 us -> 0.12 us  [placing(): jnp.einsum('ut,sbte->sbue', earlier, member.astype(jnp.bfloat16), preferr...]
    pallas_call x0 -> x4, Pallas kernels: none -> 72.4 us  [the longest x2 42.2 us: hidden_units(): pl.pallas_call(functools.partial(hidden_kernel, tp, group, cap), grid=(lo...]
    all_to_all x1, waiting for transfers between devices: 61.6 us -> 0.01 us  [move_spares(): lax.all_to_all(gate_pieces, 'ep', split_axis=1, concat_axis=1, tiled=True)]
    all_to_all x3 -> x1, waiting for transfers between devices: 116 us -> 70.1 us  [move_spares(): lax.all_to_all(chosen_gate, 'ep', split_axis=1, concat_axis=1, tiled=True)]
    all_to_all x1, waiting for transfers between devices: 31 us -> 72.6 us  [move_spares(): lax.all_to_all(chosen_up, 'ep', split_axis=1, concat_axis=1, tiled=True)]
    all_to_all x1, waiting for transfers between devices: 59.7 us -> 94.9 us  [move_spares(): lax.all_to_all(up_pieces, 'ep', split_axis=1, concat_axis=1, tiled=True)]
  transfers between devices with their start and end apart: 12 -> 10, of which waited for: 8 -> 5; matrix products, arithmetic and copies ran while one was open for 23% -> 13% of each run, Pallas kernels for 0% -> 11%
where the time goes in v1:
time: 651 us; the launch traced here: 649 us
  waiting for transfers between devices  357 us (55%)
  blocking collectives  91 us (14%)
  local copies, waits for them, and re-layouts  75.3 us (12%)
  Pallas kernels  72.4 us (11%)
  starting transfers between devices  28.4 us (4%)
  between operations  15.9 us (2%)
  other arithmetic  9.74 us (1%)
    all_to_all x1, waiting for transfers between devices, move_spares(): lax.all_to_all(up_pieces, 'ep', split_axis=1, concat_axis=1, tiled=True)  94.9 us
    all_gather x1, blocking collectives, placing(): packed = lax.all_gather(packed, 'ep')  91 us
    all_to_all x1, waiting for transfers between devices, move_spares(): lax.all_to_all(down_pieces, 'ep', split_axis=1, concat_axis=1, tiled=True)  86.1 us
    all_to_all x1, waiting for transfers between devices, move_spares(): lax.all_to_all(chosen_up, 'ep', split_axis=1, concat_axis=1, tiled=True)  72.6 us
    all_to_all x1, waiting for transfers between devices, move_spares(): lax.all_to_all(chosen_gate, 'ep', split_axis=1, concat_axis=1, tiled=True)  70.1 us
    pallas_call x2, Pallas kernels, hidden_units(): pl.pallas_call(functools.partial(hidden_kernel, tp, group, cap), grid=(lo...  42.2 us
    all_to_all x1, waiting for transfers between devices, move_spares(): lax.all_to_all(chosen_down, 'ep', split_axis=1, concat_axis=1, tiled=True)  32.2 us
    pallas_call x2, Pallas kernels, combine(): pl.pallas_call(functools.partial(combine_kernel, tp, group, cap, base is...  30.2 us
  transfers between devices with their start and end apart: 10, of which 5 were waited for; matrix products, arithmetic and copies ran while one was open for 13% of the time, Pallas kernels for 11%

profile of v1, /device:TPU:0, one launch (start us, length us, event | category | flops | bytes accessed | tf_op | source)
XLA Modules:
  0.0 649.4 jit_solution(12490695259555844191)
XLA Ops:
  11.4 3.9 constant_dynamic-slice_fusion.2
  15.2 3.2 copy.78
  21.2 7.3 %all-to-all-start.4 = ((bf16[1536,8,128]{2,0,1:T(8,128)(2,1)}), bf16[1536,8,128]{2,0,1:T(8,128)(2,1)S(1)}, u32[]{:S(2)}, u32[]{:S(2)}) async-start(bf16[1536,8,128]{2,0,1:T(8,128)(2,1)} %copy.70), calls=%async_computation.5 | async-start | bytes 6291456 | tf_op jit(solution)/shard_map/all_to_all | solution.py:219
  28.5 3.9 constant_dynamic-slice_fusion
  32.4 4.6 copy.77
  37.0 4.6 copy.67
  41.7 86.1 %all-to-all-done.4 = bf16[1536,8,128]{2,0,1:T(8,128)(2,1)S(1)} async-done(((bf16[1536,8,128]{2,0,1:T(8,128)(2,1)}), bf16[1536,8,128]{2,0,1:T(8,128)(2,1)S(1)}, u32[]{:S(2)}, u32[]{:S(2)}) %all-to-all-start.4) | async-done | bytes 3145760 | tf_op jit(solution)/shard_map/all_to_all | solution.py:219
  129.5 3.7 all-to-all-start.2
  133.2 4.0 constant_dynamic-slice_fusion.1
  137.2 4.7 copy.76
  141.9 4.6 copy.64
  146.5 94.9 %all-to-all-done.2 = bf16[384,8,512]{2,0,1:T(8,128)(2,1)S(1)} async-done(((bf16[384,8,512]{2,0,1:T(8,128)(2,1)}), bf16[384,8,512]{2,0,1:T(8,128)(2,1)S(1)}, u32[]{:S(2)}, u32[]{:S(2)}) %all-to-all-start.2) | async-done | bytes 3145760 | tf_op jit(solution)/shard_map/all_to_all | solution.py:218
  243.1 4.5 all-to-all-start
  247.6 91.0 %all-gather = f32[16,128,16]{1,2,0:T(8,128)S(1)} all-gather(f32[2,128,16]{1,2,0:T(8,128)S(1)} %pad_maximum_fusion), channel_id=2, replica_groups=mesh['ep'=8,'tp'=4] {'ep'}, dimensions={0}, use_global_device_ids=true | all-gather | bytes 147456 | tf_op jit(solution)/shard_map/all_gather | solution.py:155
  340.4 21.0 %hidden_units.3 = bf16[4,320,384]{2,1,0:T(8,128)(2,1)} custom-call(s32[2,4,4,256]{3,2,1,0:T(4,128)} %copy.61.pos_ref, bf16[32,2,128,1024]{3,2,1,0:T(8,128)(2,1)} %bitcast.48, bf16[4,384,4096]{2,1,0:T(8,128)(2,1)} %gate_ref.3, bf16[4,384,4096]{2,1,0:T(8,128)(2,1)} %up_ref.3), custom_call_target="tpu_custom_call" | custom-call | flops 8053063680 | bytes 33554432 | tf_op jit(solution)/shard_map/hidden_units/pallas_call | solution.py:57
  361.5 3.0 gather_fusion
  366.6 4.4 all-to-all-start.5
  371.3 21.2 %hidden_units.2 = bf16[4,320,384]{2,1,0:T(8,128)(2,1)} custom-call(s32[2,4,4,256]{3,2,1,0:T(4,128)} %copy.61.pos_ref, bf16[32,2,128,1024]{3,2,1,0:T(8,128)(2,1)} %bitcast.49, bf16[4,384,4096]{2,1,0:T(8,128)(2,1)} %gate_ref.3, bf16[4,384,4096]{2,1,0:T(8,128)(2,1)} %up_ref.3), custom_call_target="tpu_custom_call" | custom-call | flops 8053063680 | bytes 33554432 | tf_op jit(solution)/shard_map/hidden_units/pallas_call | solution.py:57
  395.0 4.4 gather_fusion.1
  399.4 5.6 select_bitcast_fusion
  405.0 32.2 %all-to-all-done.5 = bf16[1536,8,128]{2,0,1:T(8,128)(2,1)} async-done(((bf16[1536,8,128]{2,0,1:T(8,128)(2,1)}), bf16[1536,8,128]{2,0,1:T(8,128)(2,1)}, u32[]{:S(2)}, u32[]{:S(2)}) %all-to-all-start.5) | async-done | bytes 3145760 | tf_op jit(solution)/shard_map/all_to_all | solution.py:227
  437.2 3.7 all-to-all-start.3
  442.4 15.1 %combine.2.refs_0_ = bf16[8,2,128,1024]{3,2,1,0:T(8,128)(2,1)} custom-call(s32[2,4,256,4]{3,2,1,0:T(8,128)} %bitcast.51, f32[2,4,256,4]{3,2,1,0:T(8,128)} %bitcast.59, bf16[4,4,320,384]{3,2,1,0:T(8,128)(2,1)} %bitcast.62, bf16[4,1536,1024]{2,1,0:T(8,128)(2,1)} %down_ref.3), custom_call_target="tpu_custom_call" | custom-call | flops 4026531840 | bytes 16515072 | tf_op jit(solution)/shard_map/combine/pallas_call | solution.py:134
  457.6 15.1 %combine.3 = bf16[8,2,128,1024]{3,2,1,0:T(8,128)(2,1)} custom-call(s32[2,4,256,4]{3,2,1,0:T(8,128)} %bitcast.52, f32[2,4,256,4]{3,2,1,0:T(8,128)} %bitcast.60, bf16[4,4,320,384]{3,2,1,0:T(8,128)(2,1)} %bitcast.61, bf16[4,1536,1024]{2,1,0:T(8,128)(2,1)} %down_ref.3, bf16[8,2,128,1024]{3,2,1,0:T(8,128)(2,1)} %combine.2.refs_0_), custom_call_target="tpu_custom_call", output_to_operand_aliasing={{}: (4, {})} | custom-call | flops 4026531840 | bytes 16515072 | tf_op jit(solution)/shard_map/combine/pallas_call | solution.py:134
  472.7 72.6 %all-to-all-done.3 = bf16[384,8,512]{2,0,1:T(8,128)(2,1)S(1)} async-done(((bf16[384,8,512]{2,0,1:T(8,128)(2,1)}), bf16[384,8,512]{2,0,1:T(8,128)(2,1)S(1)}, u32[]{:S(2)}, u32[]{:S(2)}) %all-to-all-start.3) | async-done | bytes 3145760 | tf_op jit(solution)/shard_map/all_to_all | solution.py:226
  545.2 4.5 all-to-all-start.1
  549.7 4.6 copy.71
  554.4 4.7 copy.74
  561.9 4.6 copy.73
  566.5 70.1 %all-to-all-done.1 = bf16[384,8,512]{2,0,1:T(8,128)(2,1)} async-done(((bf16[384,8,512]{2,0,1:T(8,128)(2,1)}), bf16[384,8,512]{2,0,1:T(8,128)(2,1)}, u32[]{:S(2)}, u32[]{:S(2)}) %all-to-all-start.1) | async-done | bytes 3145760 | tf_op jit(solution)/shard_map/all_to_all | solution.py:225
  636.6 3.5 copy.65
  640.0 2.9 copy.72
  (50 shorter events, 19.5 us)
Async XLA Ops:
  7.2 333.2 %all-gather.8.cloned.1.call-start = ((), (), s32[]{:S(2)}) async-start(), calls=%async_computation.8 | async-start | bytes 17301504 | tf_op jit(solution)/shard_map/all_gather | solution.py:190
  21.2 106.6 %all-to-all-start.4 = ((bf16[1536,8,128]{2,0,1:T(8,128)(2,1)}), bf16[1536,8,128]{2,0,1:T(8,128)(2,1)S(1)}, u32[]{:S(2)}, u32[]{:S(2)}) async-start(bf16[1536,8,128]{2,0,1:T(8,128)(2,1)} %copy.70), calls=%async_computation.5 | async-start | bytes 6291456 | tf_op jit(solution)/shard_map/all_to_all | solution.py:219
  41.7 91.6 %copy-start.5 = (s32[2,128,8]{1,2,0:T(8,128)S(1)}, s32[2,128,8]{1,2,0:T(8,128)}, u32[]{:S(2)}) copy-start(s32[2,128,8]{1,2,0:T(8,128)} %param.11) | copy-start | bytes 24580
  127.8 1.7 copy-start.3
  129.5 111.9 %all-to-all-start.2 = ((bf16[384,8,512]{2,0,1:T(8,128)(2,1)}), bf16[384,8,512]{2,0,1:T(8,128)(2,1)S(1)}, u32[]{:S(2)}, u32[]{:S(2)}) async-start(bf16[384,8,512]{2,0,1:T(8,128)(2,1)} %copy.67), calls=%async_computation.3 | async-start | bytes 6291456 | tf_op jit(solution)/shard_map/all_to_all | solution.py:218
  141.9 4.7 copy-start.6
  146.5 192.0 %copy-start.7 = (s32[32]{0:T(128)S(1)}, s32[32]{0:T(128)}, u32[]{:S(2)}) copy-start(s32[32]{0:T(128)} %param.16) | copy-start | bytes 388
  241.4 1.7 copy-start.1
  243.1 123.5 %all-to-all-start = ((bf16[384,8,512]{2,0,1:T(8,128)(2,1)}), bf16[384,8,512]{2,0,1:T(8,128)(2,1)}, u32[]{:S(2)}, u32[]{:S(2)}) async-start(bf16[384,8,512]{2,0,1:T(8,128)(2,1)} %copy.64), calls=%async_computation.1 | async-start | bytes 6291456 | tf_op jit(solution)/shard_map/all_to_all | solution.py:217
  247.5 194.9 %all-gather.12.cloned.1.call-start = ((), (), s32[]{:S(2)}) async-start(), calls=%async_computation.10 | async-start | bytes 4915200 | tf_op jit(solution)/shard_map/all_gather | solution.py:195
  339.4 22.0 %copy-start = (s32[4,2,2,128,4]{4,3,1,0,2:T(8,128)}, s32[4,2,2,128,4]{4,3,1,0,2:T(8,128)S(1)}, u32[]{:S(2)}) copy-start(s32[4,2,2,128,4]{4,3,1,0,2:T(8,128)S(1)} %copy.59) | copy-start | bytes 98308
  366.6 70.6 %all-to-all-start.5 = ((bf16[1536,8,128]{2,0,1:T(8,128)(2,1)}), bf16[1536,8,128]{2,0,1:T(8,128)(2,1)}, u32[]{:S(2)}, u32[]{:S(2)}) async-start(bf16[1536,8,128]{2,0,1:T(8,128)(2,1)} %select_bitcast_fusion.2), calls=%async_computation.6 | async-start | bytes 6291456 | tf_op jit(solution)/shard_map/all_to_all | solution.py:227
  371.1 86.5 %all-gather.10.cloned.1.call-start = ((), (), s32[]{:S(2)}) async-start(), calls=%async_computation.9 | async-start | bytes 4915200 | tf_op jit(solution)/shard_map/all_gather | solution.py:195
  371.3 21.3 %copy-start.2 = (bf16[384,8,512]{2,0,1:T(8,128)(2,1)S(1)}, bf16[384,8,512]{2,0,1:T(8,128)(2,1)}, u32[]{:S(2)}) copy-start(bf16[384,8,512]{2,0,1:T(8,128)(2,1)} %copy-done.1) | copy-start | bytes 9437188
  395.0 4.5 copy-start.4
  437.2 108.0 %all-to-all-start.3 = ((bf16[384,8,512]{2,0,1:T(8,128)(2,1)}), bf16[384,8,512]{2,0,1:T(8,128)(2,1)S(1)}, u32[]{:S(2)}, u32[]{:S(2)}) async-start(bf16[384,8,512]{2,0,1:T(8,128)(2,1)} %get-tuple-element.21), calls=%async_computation.4 | async-start | bytes 6291456 | tf_op jit(solution)/shard_map/all_to_all | solution.py:226
  440.9 202.0 %reduce-scatter.2.cloned.1.call-start = ((), (), s32[]{:S(2)}) async-start(), calls=%async_computation.7 | async-start | bytes 4718592 | tf_op jit(solution)/shard_map/reduce_scatter | solution.py:197
  545.2 91.3 %all-to-all-start.1 = ((bf16[384,8,512]{2,0,1:T(8,128)(2,1)}), bf16[384,8,512]{2,0,1:T(8,128)(2,1)}, u32[]{:S(2)}, u32[]{:S(2)}) async-start(bf16[384,8,512]{2,0,1:T(8,128)(2,1)} %get-tuple-element.22), calls=%async_computation.2 | async-start | bytes 6291456 | tf_op jit(solution)/shard_map/all_to_all | solution.py:225
Sparse Core Ops, SparseCore 0:
  10.8 218.5 all-gather.7
  361.5 32.2 all-gather.11
  395.4 32.9 all-gather.9
  472.8 157.3 reduce-scatter.1
